TPU v7x, 512 devices: a whole 4x8x8 slice. The times are simulated.
512 devices in a mesh: band: 8 (over y), rows: 64 (over x, z, core).
Axes of the slice: x: 4, y: 8, z: 8, core: 2. Of those that a mesh axis runs over, the one named last changes fastest.
Arguments:
- start_iterate: float32 [16384, 16, 128], P(('band', 'rows')), may hold values from 0 to 2
- right_side: float32 [16384, 16, 128], P(('band', 'rows')), as said below
- diag_table: float32 [8, 128, 128], replicated, as said below
- inverse_table: float32 [8, 128, 128], replicated, as said below
- coupling_tiles: float32 [8, 128, 128], replicated, may hold values from 0 to 0.009375
- diag_index: int32 [16384], P(('band', 'rows')), may hold values from 0 to 7
- tile_index: int32 [16384, 4], P(('band', 'rows')), may hold values from 0 to 7
- source_owner: int32 [16384, 2], P(('band', 'rows')), may hold values from 0 to 63, all different within a row; in each aligned block of 32 rows (0 to 31, 32 to 63, ...) at most 2 rows name the same one
- source_local: int32 [16384, 2], P(('band', 'rows')), may hold values from 0 to 31
- aggregate_map: int32 [16384, 1], P(('band', 'rows')), may hold values from 0 to 4095
Outputs:
- swept_iterate: float32 [16384, 16, 128], P(('band', 'rows'))
Inputs may be any that keep to these rules, and one draw needn't show every extreme that they name: `source_owner`: within each aligned block of 32 rows (the rows of one device) no owner is named by more than 2 entries, a bound that some block reaches; the 2 owners of one row differ. `aggregate_map`: every aggregate is named by at least one block row. `diag_table`: diagonal entries lie from 6 to 10; off-diagonal entries are nonpositive with magnitude at most 5 / 128. `inverse_table`: entries are nonnegative; each block is a first-order approximation of the inverse of the diagonal block of the same index, not its exact inverse. `right_side`: entries are nonnegative.
All inputs are finite; a program needn't handle non-finite values.
Results may differ from a plain program's by a relative error of at most 0.0001.
Values sent between devices are 32-bit elements; how exact they have to be, the bound alone decides.
A program may use at most 64 MiB of HBM per device.

v0:
```python
import jax
import jax.numpy as jnp
from jax import lax
from jax.sharding import PartitionSpec as P

AGG_DEV = 8


HIGH = lax.Precision.HIGHEST


def shifted(value, axis, steps):
    count = lax.axis_size(axis)
    initial, last = (max(0, -steps), min(count, count - steps))
    return lax.ppermute(value, axis, [(source, source + steps) for source in range(initial, last)])


def apply_table(table, index, iterate):
    chosen = jnp.take(table, index, axis=0)
    return jnp.einsum("rst,rvt->rvs", chosen, iterate, precision=HIGH)


def coupling(iterate, wanted, slot_place, tile_mats, n_rows, capacity):
    inner = iterate.shape[1:]
    fetched = jnp.take(iterate, wanted, axis=0).reshape((n_rows, capacity) + inner)
    arrived = lax.all_to_all(fetched, "rows", split_axis=0, concat_axis=0, tiled=True)
    arrived = arrived.reshape((n_rows * capacity,) + inner)
    remote = jnp.take(arrived, slot_place, axis=0).reshape((iterate.shape[0], -1) + inner)
    from_lower = shifted(iterate, "band", 1)
    from_upper = shifted(iterate, "band", -1)
    sources = jnp.concatenate([remote, from_lower[:, None], from_upper[:, None]], axis=1)
    return jnp.einsum("rkst,rkvt->rvs", tile_mats, sources, precision=HIGH)


def on_device(
    start_iterate,
    right_side,
    diag_table,
    inverse_table,
    coupling_tiles,
    diag_index,
    tile_index,
    source_owner,
    source_local,
    aggregate_map,
):
    block_rows = start_iterate.shape[0]
    width_k = source_owner.shape[1]
    n_rows = lax.axis_size("rows")
    capacity = max(2, 2 * width_k * block_rows // n_rows)
    owners_flat = source_owner.reshape(-1)
    locals_flat = source_local.reshape(-1)
    matches = (owners_flat[:, None] == jnp.arange(n_rows, dtype=jnp.int32)[None, :]).astype(
        jnp.int32
    )
    before = jnp.cumsum(matches, axis=0) - matches
    slot_rank = jnp.sum(before * matches, axis=1)
    slot_place = owners_flat * capacity + slot_rank
    requests = jnp.zeros((n_rows * capacity,), jnp.int32).at[slot_place].set(locals_flat)
    wanted = lax.all_to_all(
        requests.reshape(n_rows, capacity), "rows", split_axis=0, concat_axis=0, tiled=True
    ).reshape(-1)
    tile_mats = jnp.take(coupling_tiles, tile_index, axis=0)
    iterate = start_iterate
    for sweep_pass in range(2):
        coupled = coupling(iterate, wanted, slot_place, tile_mats, n_rows, capacity)
        iterate = apply_table(inverse_table, diag_index, right_side + coupled)
    coupled = coupling(iterate, wanted, slot_place, tile_mats, n_rows, capacity)
    residual = right_side + coupled - apply_table(diag_table, diag_index, iterate)
    groups = aggregate_map[:, 0]
    total_groups = AGG_DEV * lax.axis_size("band") * lax.axis_size("rows")
    residual_sums = jnp.sum(residual, axis=2)
    table_sums = jnp.sum(diag_table, axis=(1, 2))
    block_sums = jnp.take(table_sums, diag_index)
    partial_residual = jax.ops.segment_sum(residual_sums, groups, num_segments=total_groups)
    partial_diag = jax.ops.segment_sum(block_sums, groups, num_segments=total_groups)
    whole_residual, whole_diag = lax.psum((partial_residual, partial_diag), ("band", "rows"))
    correction = whole_residual / whole_diag[:, None]
    return iterate + jnp.take(correction, groups, axis=0)[:, :, None]


def solution(mesh):
    in_specs = (
        P(("band", "rows"), None, None),
        P(("band", "rows"), None, None),
        P(),
        P(),
        P(),
        P(("band", "rows")),
        P(("band", "rows"), None),
        P(("band", "rows"), None),
        P(("band", "rows"), None),
        P(("band", "rows"), None),
    )
    out_specs = P(("band", "rows"), None, None)
    return jax.shard_map(
        on_device, mesh=mesh, in_specs=in_specs, out_specs=out_specs, check_vma=False
    )
```

profile of v0, /device:TPU:1, one launch (start us, length us, event | category | flops | bytes accessed | tf_op | source)
XLA Modules:
  0.0 490.1 jit_solution(2235483340600910826)
XLA Ops:
  10.5 23.9 %all_to_all.24 = s32[64,1,2]{2,1,0:T(1,128)S(1)} all-to-all(s32[64,1,2]{2,1,0:T(1,128)S(1)} %bitcast.61), channel_id=1, replica_groups=mesh['band'=8,'rows'=64] {'rows'}, dimensions={0} | all-to-all | bytes 1024 | tf_op jit(solution)/shard_map/all_to_all | solution.py:60
  38.7 5.5 %all-to-all-start.1 = ((f32[64,2,16,128]{3,2,1,0:T(8,128)}), f32[64,2,16,128]{3,2,1,0:T(8,128)}, u32[]{:S(2)}, u32[]{:S(2)}) async-start(f32[64,2,16,128]{3,2,1,0:T(8,128)} %bitcast.3), calls=%async_computation.1 | async-start | bytes 2097152 | tf_op jit(solution)/shard_map/all_to_all | solution.py:26
  44.2 3.9 collective-permute-start
  52.5 4.3 gather_fusion
  56.8 15.9 %all-to-all-done.1 = f32[64,2,16,128]{3,2,1,0:T(8,128)} async-done(((f32[64,2,16,128]{3,2,1,0:T(8,128)}), f32[64,2,16,128]{3,2,1,0:T(8,128)}, u32[]{:S(2)}, u32[]{:S(2)}) %all-to-all-start.1) | async-done | bytes 1048608 | tf_op jit(solution)/shard_map/all_to_all | solution.py:26
  72.7 2.6 gather_fusion.4
  76.5 9.3 %fusion.36 = f32[32,16,128]{2,1,0:T(8,128)S(1)} fusion(f32[32,16,128]{2,1,0:T(8,128)S(1)} %copy-done.2, f32[32,4,128,128]{3,2,1,0:T(8,128)} %bitcast.54, pred[32,4]{1,0:T(8,128)(4,1)S(1)} %copy.37, f32[32,1,16,128]{3,2,1,0:T(8,128)} %bitcast.7, f32[32,1,16,128]{3,2,1,0:T(8,128)} %bitcast.6, f32[32,2,16,128]{3,2,1,0:T(8,128)S(1)} %bitcast.60), kind=kOutput, calls=%fused_computation.38 | convolution fusion | flops 405340160 | bytes 9961600 | tf_op jit(solution)/shard_map/rkst,rkvt->rvs/dot_general | solution.py:32
  85.8 3.4 fusion.16
  91.0 2.4 broadcast_select_fusion.1
  93.4 6.5 %all-to-all-start.2 = ((f32[64,2,16,128]{3,2,1,0:T(8,128)}), f32[64,2,16,128]{3,2,1,0:T(8,128)}, u32[]{:S(2)}, u32[]{:S(2)}) async-start(f32[64,2,16,128]{3,2,1,0:T(8,128)} %bitcast.57), calls=%async_computation.2 | async-start | bytes 2097152 | tf_op jit(solution)/shard_map/all_to_all | solution.py:26
  99.9 3.9 collective-permute-start.2
  105.2 23.0 %all-to-all-done.2 = f32[64,2,16,128]{3,2,1,0:T(8,128)} async-done(((f32[64,2,16,128]{3,2,1,0:T(8,128)}), f32[64,2,16,128]{3,2,1,0:T(8,128)}, u32[]{:S(2)}, u32[]{:S(2)}) %all-to-all-start.2) | async-done | bytes 1048608 | tf_op jit(solution)/shard_map/all_to_all | solution.py:26
  128.3 2.6 gather_fusion.7
  132.1 9.5 %fusion.33 = f32[32,16,128]{2,1,0:T(8,128)S(1)} fusion(f32[32,16,128]{2,1,0:T(8,128)} %param.17, f32[32,4,128,128]{3,2,1,0:T(8,128)} %bitcast.55, pred[32,4]{1,0:T(8,128)(4,1)S(1)} %copy.37, f32[32,1,16,128]{3,2,1,0:T(8,128)} %bitcast.17, f32[32,1,16,128]{3,2,1,0:T(8,128)} %bitcast.15, f32[32,2,16,128]{3,2,1,0:T(8,128)S(1)} %bitcast.59), kind=kOutput, calls=%fused_computation.37 | convolution fusion | flops 405340160 | bytes 9961600 | tf_op jit(solution)/shard_map/rkst,rkvt->rvs/dot_general | solution.py:32
  141.6 3.4 fusion.14
  147.0 6.4 %all-to-all-start.3 = ((f32[64,2,16,128]{3,2,1,0:T(8,128)}), f32[64,2,16,128]{3,2,1,0:T(8,128)}, u32[]{:S(2)}, u32[]{:S(2)}) async-start(f32[64,2,16,128]{3,2,1,0:T(8,128)} %bitcast.22), calls=%async_computation.3 | async-start | bytes 2097152 | tf_op jit(solution)/shard_map/all_to_all | solution.py:26
  153.4 3.9 collective-permute-start.4
  159.6 22.2 %all-to-all-done.3 = f32[64,2,16,128]{3,2,1,0:T(8,128)} async-done(((f32[64,2,16,128]{3,2,1,0:T(8,128)}), f32[64,2,16,128]{3,2,1,0:T(8,128)}, u32[]{:S(2)}, u32[]{:S(2)}) %all-to-all-start.3) | async-done | bytes 1048608 | tf_op jit(solution)/shard_map/all_to_all | solution.py:26
  181.8 2.6 gather_fusion.9
  185.6 9.3 %fusion.30 = f32[32,16,128]{2,1,0:T(8,128)S(1)} fusion(f32[32,16,128]{2,1,0:T(8,128)S(1)} %copy-done.3, f32[32,4,128,128]{3,2,1,0:T(8,128)} %bitcast.56, pred[32,4]{1,0:T(8,128)(4,1)S(1)} %copy.37, f32[32,1,16,128]{3,2,1,0:T(8,128)} %bitcast.28, f32[32,1,16,128]{3,2,1,0:T(8,128)} %bitcast.26, f32[32,2,16,128]{3,2,1,0:T(8,128)S(1)} %bitcast.58), kind=kOutput, calls=%fused_computation.36 | convolution fusion | flops 405340160 | bytes 9961600 | tf_op jit(solution)/shard_map/rkst,rkvt->rvs/dot_general | solution.py:32
  194.9 3.5 fusion.39
  198.4 2.1 scatter_custom_fusion.1
  201.3 99.2 %psum.15 = f32[4096]{0:T(1024)S(1)} all-reduce(f32[4096]{0:T(1024)S(1)} %scatter_custom_fusion.2), channel_id=1, replica_groups=mesh['band'=8,'rows'=64] {'band','rows'}, use_global_device_ids=true, to_apply=%region_8.12 | all-reduce | flops 4096 | bytes 32768 | tf_op jit(solution)/shard_map/psum | solution.py:77
  300.5 179.3 %all-reduce.2.cloned.1.call-done = f32[4096,16]{1,0:T(8,128)} async-done(((f32[4096,16]{1,0:T(8,128)}), f32[4096,16]{1,0:T(8,128)}) %all-reduce.2.cloned.1.call-update) | async-done | bytes 262160 | tf_op jit(solution)/shard_map/psum | solution.py:77
  (75 shorter events, 27.5 us)
Async XLA Ops:
  6.5 45.9 %copy-start = (f32[8,128,128]{2,1,0:T(8,128)S(1)}, f32[8,128,128]{2,1,0:T(8,128)}, u32[]{:S(2)}) copy-start(f32[8,128,128]{2,1,0:T(8,128)} %param.20) | copy-start | bytes 1572868
  37.5 12.0 %copy-start.4 = (s32[32,4]{0,1:T(4,128)S(1)}, s32[32,4]{0,1:T(4,128)}, u32[]{:S(2)}) copy-start(s32[32,4]{0,1:T(4,128)} %param.22) | copy-start | bytes 1540
  37.5 12.2 %copy-start.1 = (f32[8,128,128]{2,1,0:T(8,128)S(1)}, f32[8,128,128]{2,1,0:T(8,128)}, u32[]{:S(2)}) copy-start(f32[8,128,128]{2,1,0:T(8,128)} %param.18) | copy-start | bytes 1572868
  37.5 12.3 %copy-start.5 = (s32[32]{0:T(128)S(1)}, s32[32]{0:T(128)}, u32[]{:S(2)}) copy-start(s32[32]{0:T(128)} %param.21) | copy-start | bytes 388
  38.7 34.0 %all-to-all-start.1 = ((f32[64,2,16,128]{3,2,1,0:T(8,128)}), f32[64,2,16,128]{3,2,1,0:T(8,128)}, u32[]{:S(2)}, u32[]{:S(2)}) async-start(f32[64,2,16,128]{3,2,1,0:T(8,128)} %bitcast.3), calls=%async_computation.1 | async-start | bytes 2097152 | tf_op jit(solution)/shard_map/all_to_all | solution.py:26
  44.2 32.3 %collective-permute-start = (f32[32,16,128]{2,1,0:T(8,128)}, f32[32,16,128]{2,1,0:T(8,128)}, u32[]{:S(2)}, u32[]{:S(2)}) collective-permute-start(f32[32,16,128]{2,1,0:T(8,128)} %param.16), channel_id=1, source_target_pairs={{0,64},{64,128},{128,192},{192,256},{256,320},{320,384},{384,448},... | collective-permute-start | bytes 786440 | tf_op jit(solution)/shard_map/ppermute | solution.py:15
  48.2 28.3 %collective-permute-start.1 = (f32[32,16,128]{2,1,0:T(8,128)}, f32[32,16,128]{2,1,0:T(8,128)}, u32[]{:S(2)}, u32[]{:S(2)}) collective-permute-start(f32[32,16,128]{2,1,0:T(8,128)} %param.16), channel_id=1, source_target_pairs={{64,0},{128,64},{192,128},{256,192},{320,256},{384,320},{448,384},... | collective-permute-start | bytes 786440 | tf_op jit(solution)/shard_map/ppermute | solution.py:15
  56.8 19.7 %copy-start.2 = (f32[32,16,128]{2,1,0:T(8,128)S(1)}, f32[32,16,128]{2,1,0:T(8,128)}, u32[]{:S(2)}) copy-start(f32[32,16,128]{2,1,0:T(8,128)} %param.17) | copy-start | bytes 786436
  93.4 34.9 %all-to-all-start.2 = ((f32[64,2,16,128]{3,2,1,0:T(8,128)}), f32[64,2,16,128]{3,2,1,0:T(8,128)}, u32[]{:S(2)}, u32[]{:S(2)}) async-start(f32[64,2,16,128]{3,2,1,0:T(8,128)} %bitcast.57), calls=%async_computation.2 | async-start | bytes 2097152 | tf_op jit(solution)/shard_map/all_to_all | solution.py:26
  99.9 32.2 %collective-permute-start.2 = (f32[32,16,128]{2,1,0:T(8,128)S(1)}, f32[32,16,128]{2,1,0:T(8,128)}, u32[]{:S(2)}, u32[]{:S(2)}) collective-permute-start(f32[32,16,128]{2,1,0:T(8,128)S(1)} %fusion.16), channel_id=1, source_target_pairs={{0,64},{64,128},{128,192},{192,256},{256,320},{320,384},{384,448},... | collective-permute-start | bytes 786440 | tf_op jit(solution)/shard_map/ppermute | solution.py:15
  103.8 28.3 %collective-permute-start.3 = (f32[32,16,128]{2,1,0:T(8,128)S(1)}, f32[32,16,128]{2,1,0:T(8,128)}, u32[]{:S(2)}, u32[]{:S(2)}) collective-permute-start(f32[32,16,128]{2,1,0:T(8,128)S(1)} %fusion.16), channel_id=1, source_target_pairs={{64,0},{128,64},{192,128},{256,192},{320,256},{384,320},{448,384},... | collective-permute-start | bytes 786440 | tf_op jit(solution)/shard_map/ppermute | solution.py:15
  145.8 13.1 %copy-start.6 = (s32[32,1]{0,1:T(1,128)S(1)}, s32[32,1]{0,1:T(1,128)}, u32[]{:S(2)}) copy-start(s32[32,1]{0,1:T(1,128)} %param.25) | copy-start | bytes 388
  147.0 34.8 %all-to-all-start.3 = ((f32[64,2,16,128]{3,2,1,0:T(8,128)}), f32[64,2,16,128]{3,2,1,0:T(8,128)}, u32[]{:S(2)}, u32[]{:S(2)}) async-start(f32[64,2,16,128]{3,2,1,0:T(8,128)} %bitcast.22), calls=%async_computation.3 | async-start | bytes 2097152 | tf_op jit(solution)/shard_map/all_to_all | solution.py:26
  153.4 326.5 %all-reduce.2.cloned.1.call-start = ((), (), s32[]{:S(2)}) async-start(), calls=%async_computation.4 | async-start | bytes 4194304 | tf_op jit(solution)/shard_map/psum | solution.py:77
  153.4 32.2 %collective-permute-start.4 = (f32[32,16,128]{2,1,0:T(8,128)S(1)}, f32[32,16,128]{2,1,0:T(8,128)}, u32[]{:S(2)}, u32[]{:S(2)}) collective-permute-start(f32[32,16,128]{2,1,0:T(8,128)S(1)} %fusion.14), channel_id=1, source_target_pairs={{0,64},{64,128},{128,192},{192,256},{256,320},{320,384},{384,448},... | collective-permute-start | bytes 786440 | tf_op jit(solution)/shard_map/ppermute | solution.py:15
  157.4 28.3 %collective-permute-start.5 = (f32[32,16,128]{2,1,0:T(8,128)S(1)}, f32[32,16,128]{2,1,0:T(8,128)}, u32[]{:S(2)}, u32[]{:S(2)}) collective-permute-start(f32[32,16,128]{2,1,0:T(8,128)S(1)} %fusion.14), channel_id=1, source_target_pairs={{64,0},{128,64},{192,128},{256,192},{320,256},{384,320},{448,384},... | collective-permute-start | bytes 786440 | tf_op jit(solution)/shard_map/ppermute | solution.py:15
  159.6 26.1 %copy-start.3 = (f32[32,16,128]{2,1,0:T(8,128)S(1)}, f32[32,16,128]{2,1,0:T(8,128)}, u32[]{:S(2)}) copy-start(f32[32,16,128]{2,1,0:T(8,128)} %param.17) | copy-start | bytes 786436
Sparse Core Ops, SparseCore 0:
  200.7 279.1 all-reduce.1
where the time goes:
time: 491 us; the launch traced here: 490 us
  waiting for transfers between devices  241 us (49%)
  blocking collectives  123 us (25%)
  matrix products  38.4 us (8%)
  starting transfers between devices  34.5 us (7%)
  local copies, waits for them, and re-layouts  23.8 us (5%)
  other arithmetic  16 us (3%)
  between operations  13.8 us (3%)
    psum x1, waiting for transfers between devices, on_device(): lax.psum((partial_residual, partial_diag), ('band', 'rows'))  179 us
    psum x1, blocking collectives, on_device(): lax.psum((partial_residual, partial_diag), ('band', 'rows'))  99.2 us
    all_to_all x3, waiting for transfers between devices, coupling(): lax.all_to_all(fetched, 'rows', split_axis=0, concat_axis=0, tiled=True)  61.2 us
    dot_general x3, matrix products, coupling(): return jnp.einsum('rkst,rkvt->rvs', tile_mats, sources, precision=HIGH)  28.1 us
    all_to_all x1, blocking collectives, on_device(): lax.all_to_all(requests.reshape(n_rows, capacity), 'rows', split_axis=0,...  23.9 us
    all_to_all x3, starting transfers between devices, coupling(): lax.all_to_all(fetched, 'rows', split_axis=0, concat_axis=0, tiled=True)  18.4 us
    ppermute x6, starting transfers between devices, shifted(): lax.ppermute(value, axis, [(source, source + steps) for source in range(i...  16 us
    dot_general x3, matrix products, apply_table(): return jnp.einsum('rst,rvt->rvs', chosen, iterate, precision=HIGH)  10.3 us
  transfers between devices with their start and end apart: 10, of which 4 were waited for; matrix products, arithmetic and copies ran while one was open for 4% of the time, Pallas kernels for 0%

commit v1 on v0

v1 whole, which is shorter than its diff:
```python
import functools
import jax
import jax.numpy as jnp
from jax import lax
from jax.experimental import pallas as pl
from jax.experimental.pallas import tpu as pltpu
from jax.sharding import PartitionSpec as P

MESH = pl.DeviceIdType.MESH
F32 = jnp.float32
BF16 = jnp.bfloat16
I32 = jnp.int32
PH = 128
NV = 16
NT = 8
CORES = 2
GRID_XZ = {64: (4, 8), 8: (2, 2)}


def iota(shape, dim):
    return lax.broadcasted_iota(I32, shape, dim)


def split(value):
    high = value.astype(BF16)
    return high, (value - high.astype(F32)).astype(BF16)


def nt_dot(a, b):
    return lax.dot_general(a, b, (((1,), (1,)), ((), ())), preferred_element_type=F32)


def dot(a, b):
    return jnp.dot(a, b, preferred_element_type=F32)


def kernel(
    n_band,
    n_rows,
    diag_s,
    tile_s,
    owner_s,
    local_s,
    agg_s,
    v_ref,
    rhs_ref,
    dtab,
    itab,
    ttab,
    out_ref,
    tst,
    ist,
    cols,
    colt,
    whl,
    xs,
    msg,
    recvreq,
    slots_v,
    reqs_s,
    slots_s,
    agg_row,
    meta_s,
    meta_t,
    match,
    bs_flat,
    res_flat,
    stage_a,
    stage_b,
    stage_m,
    stage_p,
    stage_o,
    send_big,
    arrived_one,
    arrived_two,
    low,
    up,
    first,
    xhl,
    send_small,
    recv_small,
    u_send,
    u_low,
    u_up,
    zbuf,
    req_sem,
    agg_sem,
    big_sem,
    band_sem,
    small_sem,
    uband_sem,
    a_sem,
    b_sem,
    loc_sem,
):
    arrived = (arrived_one, arrived_two)
    n_x, n_z = GRID_XZ[n_rows]
    n_zc = n_z * CORES
    n_xy = n_x * n_band
    block_rows = v_ref.shape[0]
    flat = block_rows * NV
    b = lax.axis_index("band")
    r = lax.axis_index("rows")
    x = r // n_zc
    zc = r % n_zc
    xy = x * n_band + b
    below = (b + n_band - 1) % n_band
    above = (b + 1) % n_band

    def zc_peer(step):
        return (b, x * n_zc + (zc + step) % n_zc)

    def xy_peer(step):
        peer = (xy + step) % n_xy
        return (peer % n_band, (peer // n_band) * n_zc + zc)

    barrier = pltpu.get_barrier_semaphore()

    def greet_rows(step, carry):
        pl.semaphore_signal(barrier, inc=1, device_id=(b, (r + step) % n_rows), device_id_type=MESH)
        return carry

    lax.fori_loop(1, n_rows, greet_rows, 0)

    def greet_planes(step, carry):
        py = (b + 1 + step // n_x) % n_band
        px = (x + step % n_x) % n_x
        pl.semaphore_signal(barrier, inc=1, device_id=(py, px * n_zc + zc), device_id_type=MESH)
        return carry

    lax.fori_loop(0, n_x * (n_band - 1), greet_planes, 0)

    sub = iota((n_rows, PH), 0)
    lane = iota((n_rows, PH), 1)
    lane1 = iota((1, PH), 1)
    parity = lane % 2
    is_local = (lane1 % 4) < 2
    lane_flat = iota((1, flat), 1) // NV

    def collect(i, carry):
        wants, count, slots, aggs, dflat, lowflat, upflat = carry
        for k in range(2):
            off = (r - owner_s[i, k] + n_rows) % n_rows
            hit = sub == off
            value = jnp.where(is_local, local_s[i, k], tile_s[i, k])
            wants = jnp.where(hit & (count == parity), value, wants)
            rank = jnp.sum(jnp.where(hit & (count > 0), 1, 0), axis=0, keepdims=True)
            slots = jnp.where(lane1 == 2 * i + k, off * 2 + jnp.clip(rank, 0, 1), slots)
            count = count + hit.astype(I32)
        here = lane_flat == i
        aggs = jnp.where(lane1 % block_rows == i, agg_s[i, 0], aggs)
        dflat = jnp.where(here, diag_s[i], dflat)
        lowflat = jnp.where(here, tile_s[i, 2], lowflat)
        upflat = jnp.where(here, tile_s[i, 3], upflat)
        return wants, count, slots, aggs, dflat, lowflat, upflat

    zero_rows = jnp.zeros((n_rows, PH), I32)
    zero_row = jnp.zeros((1, PH), I32)
    zero_flat = jnp.zeros((1, flat), I32)
    wants, _, slots, aggs, dflat, lowflat, upflat = lax.fori_loop(
        0, block_rows, collect, (zero_rows, zero_rows, zero_row, zero_row, zero_flat, zero_flat, zero_flat)
    )
    for off in range(n_rows):
        msg[off] = wants[off : off + 1, :]
    recvreq[0] = wants[0:1, :]
    slots_v[0] = slots
    agg_row[0] = aggs.astype(F32)
    meta_s[pl.ds(zc, 1)] = aggs.astype(F32)[None]
    meta_t[pl.ds(xy, 1)] = aggs.astype(F32)[None]
    slot_copy = pltpu.make_async_copy(slots_v, slots_s, loc_sem.at[0])
    slot_copy.start()

    col_t = jnp.concatenate([jnp.sum(ttab[t], axis=0, keepdims=True) for t in range(NT)], axis=0)
    col_d = jnp.concatenate([jnp.sum(dtab[t], axis=0, keepdims=True) for t in range(NT)], axis=0)
    for t in range(NT):
        colt[t] = col_t[t : t + 1, :]
    cols[...] = jnp.concatenate(split(col_t) + split(col_d), axis=0)
    table_sum = jnp.sum(col_d, axis=1, keepdims=True)
    sub8 = iota((NT, flat), 0)
    block_sum = jnp.sum(jnp.where(sub8 == dflat, table_sum, 0.0), axis=0, keepdims=True)
    for q in range(4):
        bs_flat[0, q : q + 1, :] = block_sum[:, q * PH : (q + 1) * PH]
    stage_a[0, pl.ds(zc, 1)] = bs_flat[...]

    pl.semaphore_wait(barrier, n_rows - 1 + n_x * (n_band - 1))

    def rows_copies(source, target, width, sems, step_sign):
        def copy(step):
            peer = (r + step_sign * step + n_rows) % n_rows
            return pltpu.make_async_remote_copy(
                src_ref=source(step),
                dst_ref=target.at[pl.ds(step * width, width)],
                send_sem=sems.at[0],
                recv_sem=sems.at[1],
                device_id=(b, peer),
                device_id_type=MESH,
            )

        def start(step, carry):
            copy(step).start()
            return carry

        lax.fori_loop(1, n_rows, start, 0)

    def drain(ref, count, sems):
        part = ref.at[pl.ds(0, count)]
        pltpu.make_async_copy(part, part, sems.at[0]).wait()

    def arrive(ref, count, sems):
        part = ref.at[pl.ds(0, count)]
        pltpu.make_async_copy(part, part, sems.at[1]).wait()

    def band_copies(source, to_above, to_below, sems):
        copies = []
        for side, (target, peer) in enumerate(((to_above, above), (to_below, below))):
            copy = pltpu.make_async_remote_copy(
                src_ref=source,
                dst_ref=target,
                send_sem=sems.at[side, 0],
                recv_sem=sems.at[side, 1],
                device_id=(peer, r),
                device_id_type=MESH,
            )
            copy.start()
            copies.append(copy)
        return copies

    rows_copies(lambda step: msg.at[pl.ds(step, 1)], recvreq, 1, req_sem, -1)

    def group_copies(source, target, index, peer_of, count, sems):
        def start(step, carry):
            pltpu.make_async_remote_copy(
                src_ref=source(step),
                dst_ref=target.at[pl.ds(index, 1)],
                send_sem=sems.at[0],
                recv_sem=sems.at[1],
                device_id=peer_of(step),
                device_id_type=MESH,
            ).start()
            return carry

        lax.fori_loop(1, count, start, 0)

    group_copies(lambda step: agg_row, meta_s, zc, zc_peer, n_zc, agg_sem.at[0])
    group_copies(lambda step: agg_row, meta_t, xy, xy_peer, n_xy, agg_sem.at[1])
    group_copies(lambda step: bs_flat, stage_a.at[0], zc, zc_peer, n_zc, a_sem.at[0])
    band1 = band_copies(v_ref, low.at[0], up.at[0], band_sem.at[0])

    def prepare(t, carry):
        rows = pl.ds(pl.multiple_of(t * PH, PH), PH)
        for source, target in ((ttab, tst), (itab, ist)):
            high, rest = split(jnp.transpose(source[t]))
            target[rows, 0:PH] = high
            target[rows, PH : 2 * PH] = rest
        return carry

    arrive(recvreq, n_rows - 1, req_sem)
    req_copy = pltpu.make_async_copy(recvreq, reqs_s, loc_sem.at[1])
    req_copy.start()
    slot_copy.wait()
    req_copy.wait()

    def send_blocks(source, which):
        def gather(off, carry):
            for rank in range(2):
                send_big[which, 2 * off + rank] = source[reqs_s[off, 0, rank]]
            return carry

        lax.fori_loop(0, n_rows, gather, 0)
        arrived[which][0:2] = send_big[which, 0:2]
        rows_copies(
            lambda step: send_big.at[which].at[pl.ds(2 * step, 2)],
            arrived[which],
            2,
            big_sem.at[which],
            1,
        )

    send_blocks(v_ref, 0)
    lax.fori_loop(0, NT, prepare, 0)

    def coupled_apply(which, target):
        def form(i, carry):
            rows = pl.ds(pl.multiple_of(i * NV, NV), NV)
            rest_rows = pl.ds(pl.multiple_of(flat + i * NV, NV), NV)
            sources = (
                arrived[which][slots_s[0, 0, 2 * i]],
                arrived[which][slots_s[0, 0, 2 * i + 1]],
                low[which, i],
                up[which, i],
            )
            tiles = (
                tile_s[i, 0],
                tile_s[i, 1],
                jnp.where(b == 0, -1, tile_s[i, 2]),
                jnp.where(b == n_band - 1, -1, tile_s[i, 3]),
            )
            for t in range(NT):
                total = jnp.where(tiles[0] == t, 1.0, 0.0) * sources[0]
                for k in range(1, 4):
                    total = total + jnp.where(tiles[k] == t, 1.0, 0.0) * sources[k]
                high, rest = split(total)
                whl[rows, t * PH : (t + 1) * PH] = high
                whl[rest_rows, t * PH : (t + 1) * PH] = rest
            return carry

        lax.fori_loop(0, block_rows, form, 0)
        y = dot(whl[...], tst[...])
        y = y[:flat] + y[flat:]
        xs[...] = rhs_ref[...].reshape(flat, PH) + (y[:, :PH] + y[:, PH:])

        def form_diag(i, carry):
            rows = pl.ds(pl.multiple_of(i * NV, NV), NV)
            rest_rows = pl.ds(pl.multiple_of(flat + i * NV, NV), NV)
            value = xs[rows, :]
            rest = value - value.astype(BF16).astype(F32)
            for t in range(NT):
                keep = jnp.where(diag_s[i] == t, 1.0, 0.0)
                whl[rows, t * PH : (t + 1) * PH] = (value * keep).astype(BF16)
                whl[rest_rows, t * PH : (t + 1) * PH] = (rest * keep).astype(BF16)
            return carry

        lax.fori_loop(0, block_rows, form_diag, 0)
        y = dot(whl[...], ist[...])
        y = y[:flat] + y[flat:]
        target[...] = (y[:, :PH] + y[:, PH:]).reshape(block_rows, NV, PH)

    arrive(meta_s, n_zc - 1, agg_sem.at[0])
    arrive(meta_t, n_xy - 1, agg_sem.at[1])
    lanes = iota((1, PH), 1)
    per_row = PH // block_rows
    pieces = []
    for group in range(n_zc // per_row):
        piece = jnp.zeros((1, PH), F32)
        for place in range(per_row):
            piece = jnp.where(lanes // block_rows == place, meta_s[group * per_row + place], piece)
        pieces.append(piece)
    source_row = jnp.concatenate(pieces, axis=1)
    own_lane = iota((block_rows, PH), 1) == iota((block_rows, PH), 0)

    def build(d, carry):
        column = jnp.sum(jnp.where(own_lane, meta_t[d], 0.0), axis=1, keepdims=True)
        rows = pl.ds(pl.multiple_of(d * block_rows, block_rows), block_rows)
        match[rows, :] = jnp.where(column == source_row, 1.0, 0.0).astype(BF16)
        return carry

    lax.fori_loop(0, n_xy, build, 0)
    block_lane = (iota((8, PH), 1) // NV) == iota((8, PH), 0)
    fold = jnp.where(iota((PH, PH), 0) % NV == iota((PH, PH), 1) % NV, 1.0, 0.0).astype(BF16)

    def fold_lanes(value):
        high, rest = split(value)
        return dot(high, fold) + dot(rest, fold)

    def to_flat_rows(value, q):
        picked = jnp.where(block_lane, value[q * 8 : (q + 1) * 8, :], 0.0)
        return jnp.sum(picked, axis=0, keepdims=True)

    def partial_sums(which):
        arrive(stage_a.at[which], n_zc - 1, a_sem.at[which])

        def spread(source, carry):
            value = stage_a[which, source]
            for q in range(4):
                rows = pl.ds(pl.multiple_of(source * block_rows + q * 8, 8), 8)
                stage_m[rows, :] = jnp.where(block_lane, value[q : q + 1, :], 0.0)
            return carry

        lax.fori_loop(0, n_zc, spread, 0)
        both = jnp.concatenate(split(stage_m[...]), axis=1)
        y = dot(match[...], both)
        stage_p[...] = fold_lanes(y[:, :PH] + y[:, PH:])

        def flatten(d, carry):
            value = stage_p[pl.ds(pl.multiple_of(d * block_rows, block_rows), block_rows), :]
            for q in range(4):
                stage_o[which, d, q : q + 1, :] = to_flat_rows(value, q)
            return carry

        lax.fori_loop(0, n_xy, flatten, 0)
        stage_b[which, pl.ds(xy, 1)] = stage_o[which, pl.ds(xy, 1)]

        def out_part(step):
            return stage_o.at[which].at[pl.ds((xy + step) % n_xy, 1)]

        group_copies(out_part, stage_b.at[which], xy, xy_peer, n_xy, b_sem.at[which])

    partial_sums(0)

    arrive(arrived[0], 2 * (n_rows - 1), big_sem.at[0])
    for copy in band1:
        copy.wait_recv()
    coupled_apply(0, first)
    send_blocks(first, 1)
    band2 = band_copies(first, low.at[1], up.at[1], band_sem.at[1])
    ones = jnp.ones((8, PH), BF16)
    rhs_parts = split(rhs_ref[...].reshape(flat, PH))
    rhs_sum = (nt_dot(ones, rhs_parts[0]) + nt_dot(ones, rhs_parts[1]))[0:1, :]
    arrive(arrived[1], 2 * (n_rows - 1), big_sem.at[1])
    for copy in band2:
        copy.wait_recv()
    coupled_apply(1, out_ref)

    second_parts = split(out_ref[...].reshape(flat, PH))
    projected = nt_dot(cols[...], second_parts[0]) + nt_dot(cols[...], second_parts[1])
    u_send[...] = projected[0:8] + projected[8:16]
    uband = band_copies(u_send, u_low, u_up, uband_sem)

    def edge(off, carry):
        for rank in range(2):
            value = out_ref[reqs_s[off, 0, rank]] * colt[reqs_s[off, 0, 2 + rank]]
            high, rest = split(value)
            place = pl.ds(pl.multiple_of((2 * off + rank) * NV, NV), NV)
            xhl[0, place, :] = high
            xhl[1, place, :] = rest
        return carry

    lax.fori_loop(0, n_rows, edge, 0)
    edges = nt_dot(ones, xhl[0]) + nt_dot(ones, xhl[1])
    for group in range(n_rows // 4):
        send_small[group] = edges[0:1, group * PH : (group + 1) * PH]
    recv_small[0] = edges[0:1, 0:PH]
    rows_copies(lambda step: send_small.at[pl.ds(step // 4, 1)], recv_small, 1, small_sem, 1)

    own = projected[16:24] + projected[24:32]
    local_sum = rhs_sum - jnp.sum(jnp.where(sub8 == dflat, own, 0.0), axis=0, keepdims=True)
    for copy in uband:
        copy.wait_recv()
    has_low = jnp.where(b == 0, 0.0, 1.0)
    has_up = jnp.where(b == n_band - 1, 0.0, 1.0)
    local_sum = local_sum + has_low * jnp.sum(
        jnp.where(sub8 == lowflat, u_low[...], 0.0), axis=0, keepdims=True
    )
    local_sum = local_sum + has_up * jnp.sum(
        jnp.where(sub8 == upflat, u_up[...], 0.0), axis=0, keepdims=True
    )
    arrive(recv_small, n_rows - 1, small_sem)

    def collect_edges(i, carry):
        total = jnp.zeros((1, PH), F32)
        for k in range(2):
            slot = slots_s[0, 0, 2 * i + k]
            piece = recv_small[slot // 2]
            total = total + jnp.where(lanes // NV == slot % 8, piece, 0.0)
        zbuf[i] = total
        return carry

    lax.fori_loop(0, block_rows, collect_edges, 0)
    rows_of = fold_lanes(zbuf[...].reshape(block_rows, PH))
    for q in range(4):
        res_flat[0, q : q + 1, :] = local_sum[:, q * PH : (q + 1) * PH] + to_flat_rows(rows_of, q)
    stage_a[1, pl.ds(zc, 1)] = res_flat[...]
    group_copies(lambda step: res_flat, stage_a.at[1], zc, zc_peer, n_zc, a_sem.at[1])
    partial_sums(1)

    arrive(stage_b.at[0], n_xy - 1, b_sem.at[0])
    denominator = jnp.sum(stage_b[0], axis=0)
    arrive(stage_b.at[1], n_xy - 1, b_sem.at[1])
    correction = jnp.sum(stage_b[1], axis=0) / denominator
    eye = iota((PH, PH), 0) == iota((PH, PH), 1)
    for q in range(4):
        column = jnp.sum(jnp.where(eye, correction[q : q + 1, :], 0.0), axis=1, keepdims=True)
        out_ref[q * 8 : (q + 1) * 8] = out_ref[q * 8 : (q + 1) * 8] + column.reshape(8, NV, 1)

    drain(msg, n_rows - 1, req_sem)
    drain(meta_s, n_zc - 1, agg_sem.at[0])
    drain(meta_t, n_xy - 1, agg_sem.at[1])
    for which in range(2):
        drain(send_big.at[which], 2 * (n_rows - 1), big_sem.at[which])
        drain(stage_a.at[which], n_zc - 1, a_sem.at[which])
        drain(stage_o.at[which], n_xy - 1, b_sem.at[which])
    drain(recv_small, n_rows - 1, small_sem)
    for copy in band1 + band2 + uband:
        copy.wait_send()


def on_device(
    start_iterate,
    right_side,
    diag_table,
    inverse_table,
    coupling_tiles,
    diag_index,
    tile_index,
    source_owner,
    source_local,
    aggregate_map,
):
    n_band = lax.axis_size("band")
    n_rows = lax.axis_size("rows")
    block_rows = start_iterate.shape[0]
    n_x, n_z = GRID_XZ[n_rows]
    n_zc, n_xy = n_z * CORES, n_x * n_band
    flat = block_rows * NV
    vmem = pltpu.VMEM
    dma = pltpu.SemaphoreType.DMA
    smem = pl.BlockSpec(memory_space=pltpu.SMEM)
    full = pl.BlockSpec(memory_space=pltpu.VMEM)
    scratch = [
        vmem((NT * PH, 2 * PH), BF16),
        vmem((NT * PH, 2 * PH), BF16),
        vmem((4 * NT, PH), BF16),
        vmem((NT, 1, PH), F32),
        vmem((2 * flat, NT * PH), BF16),
        vmem((flat, PH), F32),
        vmem((n_rows, 1, PH), I32),
        vmem((n_rows, 1, PH), I32),
        vmem((1, 1, PH), I32),
        pltpu.SMEM((n_rows, 1, PH), I32),
        pltpu.SMEM((1, 1, PH), I32),
        vmem((1, 1, PH), F32),
        vmem((n_zc, 1, PH), F32),
        vmem((n_xy, 1, PH), F32),
        vmem((n_xy * block_rows, n_zc * block_rows), BF16),
        vmem((1, 4, PH), F32),
        vmem((1, 4, PH), F32),
        vmem((2, n_zc, 4, PH), F32),
        vmem((2, n_xy, 4, PH), F32),
        vmem((n_zc * block_rows, PH), F32),
        vmem((n_xy * block_rows, PH), F32),
        vmem((2, n_xy, 4, PH), F32),
        vmem((2, 2 * n_rows, NV, PH), F32),
        vmem((2 * n_rows, NV, PH), F32),
        vmem((2 * n_rows, NV, PH), F32),
        vmem((2, block_rows, NV, PH), F32),
        vmem((2, block_rows, NV, PH), F32),
        vmem((block_rows, NV, PH), F32),
        vmem((2, 2 * n_rows * NV, PH), BF16),
        vmem((n_rows // 4, 1, PH), F32),
        vmem((n_rows, 1, PH), F32),
        vmem((NT, flat), F32),
        vmem((NT, flat), F32),
        vmem((NT, flat), F32),
        vmem((block_rows, 1, PH), F32),
        dma((2,)),
        dma((2, 2)),
        dma((2, 2)),
        dma((2, 2, 2)),
        dma((2,)),
        dma((2, 2)),
        dma((2, 2)),
        dma((2, 2)),
        dma((2,)),
    ]
    return pl.pallas_call(
        functools.partial(kernel, n_band, n_rows),
        out_shape=jax.ShapeDtypeStruct(start_iterate.shape, F32),
        in_specs=[smem] * 5 + [full] * 5,
        out_specs=full,
        scratch_shapes=scratch,
        compiler_params=pltpu.CompilerParams(
            collective_id=0, has_side_effects=True, vmem_limit_bytes=48 * 1024 * 1024
        ),
    )(
        diag_index,
        tile_index,
        source_owner,
        source_local,
        aggregate_map,
        start_iterate,
        right_side,
        diag_table,
        inverse_table,
        coupling_tiles,
    )


def solution(mesh):
    in_specs = (
        P(("band", "rows"), None, None),
        P(("band", "rows"), None, None),
        P(),
        P(),
        P(),
        P(("band", "rows")),
        P(("band", "rows"), None),
        P(("band", "rows"), None),
        P(("band", "rows"), None),
        P(("band", "rows"), None),
    )
    out_specs = P(("band", "rows"), None, None)
    return jax.shard_map(
        on_device, mesh=mesh, in_specs=in_specs, out_specs=out_specs, check_vma=False
    )
```

time: 491 us -> 116 us (0.24)
  waiting for transfers between devices: 241 us -> 0 us
  blocking collectives: 123 us -> 0 us
  Pallas kernels: 0 us -> 108 us
  matrix products: 38.4 us -> 0 us
  starting transfers between devices: 34.5 us -> 0 us
  other arithmetic: 16 us -> 0 us
  local copies, waits for them, and re-layouts: 23.8 us -> 8.49 us
  between operations: 13.8 us -> 0.02 us
    psum x1 -> x0, waiting for transfers between devices: 179 us -> none  [on_device(): lax.psum((partial_residual, partial_diag), ('band', 'rows'))]
    pallas_call x0 -> x1, Pallas kernels: none -> 108 us  [on_device(): pl.pallas_call(functools.partial(kernel, n_band, n_rows), out_shape=jax.S...]
    psum x1 -> x0, blocking collectives: 99.2 us -> none  [on_device(): lax.psum((partial_residual, partial_diag), ('band', 'rows'))]
    all_to_all x3 -> x0, waiting for transfers between devices: 61.2 us -> none  [coupling(): lax.all_to_all(fetched, 'rows', split_axis=0, concat_axis=0, tiled=True)]
    dot_general x6 -> x0, matrix products: 38.4 us -> none  [the longest x3 28.1 us: coupling(): return jnp.einsum('rkst,rkvt->rvs', tile_mats, sources, precision=HIGH)]
    all_to_all x1 -> x0, blocking collectives: 23.9 us -> none  [on_device(): lax.all_to_all(requests.reshape(n_rows, capacity), 'rows', split_axis=0,...]
    gather x11 -> x0, local copies, waits for them, and re-layouts: 19.9 us -> none  [the longest x3 7.83 us: coupling(): jnp.take(arrived, slot_place, axis=0)]
    all_to_all x3 -> x0, starting transfers between devices: 18.4 us -> none  [coupling(): lax.all_to_all(fetched, 'rows', split_axis=0, concat_axis=0, tiled=True)]
  transfers between devices with their start and end apart: 10 -> 0, of which waited for: 4 -> 0; matrix products, arithmetic and copies ran while one was open for 4% -> 0% of each run, Pallas kernels for 0% -> 0%
where the time goes in v1:
time: 116 us
  Pallas kernels  108 us (93%)
  local copies, waits for them, and re-layouts  8.49 us (7%)
    pallas_call x1, Pallas kernels, on_device(): pl.pallas_call(functools.partial(kernel, n_band, n_rows), out_shape=jax.S...  108 us
    unnamed x23, local copies, waits for them, and re-layouts  8.49 us

profile of v1, /device:TPU:1, one launch (start us, length us, event | category | flops | bytes accessed | tf_op | source)
XLA Modules:
  0.0 116.1 jit_solution(16039793250567651201)
XLA Ops:
  0.0 0.0 copy-start.6
  0.0 0.8 copy.11.tile_s
  0.8 0.0 copy-done.6
  0.8 0.0 copy-start.7
  0.8 0.1 copy.12.owner_s
  0.9 0.6 copy-done.7
  1.5 0.0 copy-start.8
  1.5 0.1 copy.13.local_s
  1.6 0.6 copy-done.8
  2.1 0.0 copy-start.5
  2.1 0.1 copy.14.agg_s
  2.2 0.6 copy-done.5
  2.8 0.0 copy-start
  2.8 1.0 copy-done
  3.8 0.0 copy-start.1
  3.8 1.0 copy-done.1
  4.9 0.0 copy-start.2
  4.9 1.0 copy-done.2
  5.9 0.0 copy-start.3
  5.9 0.9 copy-done.3
  6.8 0.0 copy-start.4
  6.9 0.9 copy-done.4
  7.8 107.6 %shard_map.100 = f32[32,16,128]{2,1,0:T(8,128)S(1)} custom-call(s32[32]{0:T(128)S(1)} %copy-done.5, s32[32,4]{1,0:T(8,128)S(1)} %copy.11.tile_s, s32[32,2]{1,0:T(8,128)S(1)} %copy.12.owner_s, s32[32,2]{1,0:T(8,128)S(1)} %copy.13.local_s, s32[32,1]{1,0:T(8,128)S(1)} %copy.14.agg_s, f32[32,16,128]{2,1,0:T(8,128)S(1)} %copy-done.3, ...), custom_call_target="tpu_custom_call" | custom-call | tf_op jit(solution)/shard_map/pallas_call | solution.py:545
  115.4 0.7 copy.16
Async XLA Ops:
  0.0 0.8 copy-start.6
  0.8 0.7 copy-start.7
  1.5 0.7 copy-start.8
  2.1 0.7 copy-start.5
  2.8 1.0 copy-start
  3.8 1.0 copy-start.1
  4.9 1.0 copy-start.2
  5.9 0.9 copy-start.3
  6.8 0.9 copy-start.4

commit v2 on v1

--- a/solution.py
+++ b/solution.py
@@ -12,6 +12,8 @@
 I32 = jnp.int32
 PH = 128
 NV = 16
+HALF = 8
+PARTS = NV // HALF
 NT = 8
 CORES = 2
 GRID_XZ = {64: (4, 8), 8: (2, 2)}
@@ -19,6 +21,10 @@
 
 def iota(shape, dim):
     return lax.broadcasted_iota(I32, shape, dim)
+
+
+def best(trips):
+    return max(n for n in range(1, 10) if trips % n == 0)
 
 
 def split(value):
@@ -42,12 +48,17 @@
     owner_s,
     local_s,
     agg_s,
-    v_ref,
+    v_hbm,
+    rhs_hbm,
+    dtab_hbm,
+    itab_hbm,
+    ttab_hbm,
+    out_ref,
     rhs_ref,
     dtab,
     itab,
     ttab,
-    out_ref,
+    in_sem,
     tst,
     ist,
     cols,
@@ -71,11 +82,16 @@
     stage_p,
     stage_o,
     send_big,
-    arrived_one,
-    arrived_two,
+    arrived_00,
+    arrived_01,
+    arrived_10,
+    arrived_11,
     low,
     up,
-    first,
+    field_00,
+    field_01,
+    field_10,
+    field_11,
     xhl,
     send_small,
     recv_small,
@@ -93,11 +109,12 @@
     b_sem,
     loc_sem,
 ):
-    arrived = (arrived_one, arrived_two)
+    arrived = ((arrived_00, arrived_01), (arrived_10, arrived_11))
+    field = ((field_00, field_01), (field_10, field_11))
     n_x, n_z = GRID_XZ[n_rows]
     n_zc = n_z * CORES
     n_xy = n_x * n_band
-    block_rows = v_ref.shape[0]
+    block_rows = v_hbm.shape[0]
     flat = block_rows * NV
     b = lax.axis_index("band")
     r = lax.axis_index("rows")
@@ -108,27 +125,43 @@
     above = (b + 1) % n_band
 
     def zc_peer(step):
-        return (b, x * n_zc + (zc + step) % n_zc)
+        return (b, x * n_zc + lax.rem(zc + step, n_zc))
 
     def xy_peer(step):
-        peer = (xy + step) % n_xy
-        return (peer % n_band, (peer // n_band) * n_zc + zc)
+        peer = lax.rem(xy + step, n_xy)
+        return (lax.rem(peer, n_band), lax.div(peer, n_band) * n_zc + zc)
+
+    loads = [
+        pltpu.make_async_copy(source, target, in_sem.at[n])
+        for n, (source, target) in enumerate(
+            (
+                (v_hbm.at[:, 0:HALF, :], field_00),
+                (v_hbm.at[:, HALF:NV, :], field_01),
+                (ttab_hbm, ttab),
+                (dtab_hbm, dtab),
+                (itab_hbm, itab),
+                (rhs_hbm, rhs_ref),
+            )
+        )
+    ]
+    for load in loads:
+        load.start()
 
     barrier = pltpu.get_barrier_semaphore()
 
     def greet_rows(step, carry):
-        pl.semaphore_signal(barrier, inc=1, device_id=(b, (r + step) % n_rows), device_id_type=MESH)
+        pl.semaphore_signal(barrier, inc=1, device_id=(b, lax.rem(r + step, n_rows)), device_id_type=MESH)
         return carry
 
-    lax.fori_loop(1, n_rows, greet_rows, 0)
+    lax.fori_loop(1, n_rows, greet_rows, 0, unroll=best(n_rows - 1))
 
     def greet_planes(step, carry):
-        py = (b + 1 + step // n_x) % n_band
-        px = (x + step % n_x) % n_x
+        py = lax.rem(b + 1 + lax.div(step, n_x), n_band)
+        px = lax.rem(x + step, n_x)
         pl.semaphore_signal(barrier, inc=1, device_id=(py, px * n_zc + zc), device_id_type=MESH)
         return carry
 
-    lax.fori_loop(0, n_x * (n_band - 1), greet_planes, 0)
+    lax.fori_loop(0, n_x * (n_band - 1), greet_planes, 0, unroll=best(n_x * (n_band - 1)))
 
     sub = iota((n_rows, PH), 0)
     lane = iota((n_rows, PH), 1)
@@ -140,18 +173,18 @@
     def collect(i, carry):
         wants, count, slots, aggs, dflat, lowflat, upflat = carry
         for k in range(2):
-            off = (r - owner_s[i, k] + n_rows) % n_rows
+            off = lax.rem(r - owner_s[k, i] + n_rows, n_rows)
             hit = sub == off
-            value = jnp.where(is_local, local_s[i, k], tile_s[i, k])
+            value = jnp.where(is_local, local_s[k, i], tile_s[k, i])
             wants = jnp.where(hit & (count == parity), value, wants)
             rank = jnp.sum(jnp.where(hit & (count > 0), 1, 0), axis=0, keepdims=True)
             slots = jnp.where(lane1 == 2 * i + k, off * 2 + jnp.clip(rank, 0, 1), slots)
             count = count + hit.astype(I32)
         here = lane_flat == i
-        aggs = jnp.where(lane1 % block_rows == i, agg_s[i, 0], aggs)
+        aggs = jnp.where(lane1 % block_rows == i, agg_s[0, i], aggs)
         dflat = jnp.where(here, diag_s[i], dflat)
-        lowflat = jnp.where(here, tile_s[i, 2], lowflat)
-        upflat = jnp.where(here, tile_s[i, 3], upflat)
+        lowflat = jnp.where(here, tile_s[2, i], lowflat)
+        upflat = jnp.where(here, tile_s[3, i], upflat)
         return wants, count, slots, aggs, dflat, lowflat, upflat
 
     zero_rows = jnp.zeros((n_rows, PH), I32)
@@ -170,6 +203,8 @@
     slot_copy = pltpu.make_async_copy(slots_v, slots_s, loc_sem.at[0])
     slot_copy.start()
 
+    for load in loads[:4]:
+        load.wait()
     col_t = jnp.concatenate([jnp.sum(ttab[t], axis=0, keepdims=True) for t in range(NT)], axis=0)
     col_d = jnp.concatenate([jnp.sum(dtab[t], axis=0, keepdims=True) for t in range(NT)], axis=0)
     for t in range(NT):
@@ -186,7 +221,7 @@
 
     def rows_copies(source, target, width, sems, step_sign):
         def copy(step):
-            peer = (r + step_sign * step + n_rows) % n_rows
+            peer = lax.rem(r + step_sign * step + n_rows, n_rows)
             return pltpu.make_async_remote_copy(
                 src_ref=source(step),
                 dst_ref=target.at[pl.ds(step * width, width)],
@@ -200,7 +235,7 @@
             copy(step).start()
             return carry
 
-        lax.fori_loop(1, n_rows, start, 0)
+        lax.fori_loop(1, n_rows, start, 0, unroll=best(n_rows - 1))
 
     def drain(ref, count, sems):
         part = ref.at[pl.ds(0, count)]
@@ -239,12 +274,21 @@
             ).start()
             return carry
 
-        lax.fori_loop(1, count, start, 0)
+        lax.fori_loop(1, count, start, 0, unroll=best(count - 1))
 
     group_copies(lambda step: agg_row, meta_s, zc, zc_peer, n_zc, agg_sem.at[0])
     group_copies(lambda step: agg_row, meta_t, xy, xy_peer, n_xy, agg_sem.at[1])
     group_copies(lambda step: bs_flat, stage_a.at[0], zc, zc_peer, n_zc, a_sem.at[0])
-    band1 = band_copies(v_ref, low.at[0], up.at[0], band_sem.at[0])
+
+    def share_band(which, part):
+        return band_copies(
+            field[which][part],
+            low.at[which].at[part],
+            up.at[which].at[part],
+            band_sem.at[which].at[part],
+        )
+
+    bands = [[share_band(0, part) for part in range(PARTS)], []]
 
     def prepare(t, carry):
         rows = pl.ds(pl.multiple_of(t * PH, PH), PH)
@@ -260,70 +304,91 @@
     slot_copy.wait()
     req_copy.wait()
 
-    def send_blocks(source, which):
+    def send_blocks(which, part):
+        source = field[which][part]
+        buffer = send_big.at[which].at[part]
+
         def gather(off, carry):
             for rank in range(2):
-                send_big[which, 2 * off + rank] = source[reqs_s[off, 0, rank]]
+                buffer[2 * off + rank] = source[reqs_s[off, 0, rank]]
             return carry
 
-        lax.fori_loop(0, n_rows, gather, 0)
-        arrived[which][0:2] = send_big[which, 0:2]
+        lax.fori_loop(0, n_rows, gather, 0, unroll=4)
+        arrived[which][part][0:2] = buffer[0:2]
         rows_copies(
-            lambda step: send_big.at[which].at[pl.ds(2 * step, 2)],
-            arrived[which],
+            lambda step: buffer.at[pl.ds(2 * step, 2)],
+            arrived[which][part],
             2,
-            big_sem.at[which],
+            big_sem.at[which].at[part],
             1,
         )
 
-    send_blocks(v_ref, 0)
+    for part in range(PARTS):
+        send_blocks(0, part)
+    for load in loads[4:]:
+        load.wait()
     lax.fori_loop(0, NT, prepare, 0)
-
-    def coupled_apply(which, target):
-        def form(i, carry):
-            rows = pl.ds(pl.multiple_of(i * NV, NV), NV)
-            rest_rows = pl.ds(pl.multiple_of(flat + i * NV, NV), NV)
-            sources = (
-                arrived[which][slots_s[0, 0, 2 * i]],
-                arrived[which][slots_s[0, 0, 2 * i + 1]],
-                low[which, i],
-                up[which, i],
-            )
-            tiles = (
-                tile_s[i, 0],
-                tile_s[i, 1],
-                jnp.where(b == 0, -1, tile_s[i, 2]),
-                jnp.where(b == n_band - 1, -1, tile_s[i, 3]),
-            )
+    size = block_rows * HALF
+
+    def coupled_apply(which, part, target):
+        arrive(arrived[which][part], 2 * (n_rows - 1), big_sem.at[which].at[part])
+        for copy in bands[which][part]:
+            copy.wait_recv()
+        columns = slice(part * HALF, (part + 1) * HALF)
+
+        def form(pair, carry):
+            rows = pl.ds(pl.multiple_of(pair * NV, NV), NV)
+            rest_rows = pl.ds(pl.multiple_of(size + pair * NV, NV), NV)
+            sums = []
+            for i in (2 * pair, 2 * pair + 1):
+                sources = (
+                    arrived[which][part][slots_s[0, 0, 2 * i]],
+                    arrived[which][part][slots_s[0, 0, 2 * i + 1]],
+                    low[which, part, i],
+                    up[which, part, i],
+                )
+                tiles = (
+                    tile_s[0, i],
+                    tile_s[1, i],
+                    jnp.where(b == 0, -1, tile_s[2, i]),
+                    jnp.where(b == n_band - 1, -1, tile_s[3, i]),
+                )
+                totals = []
+                for t in range(NT):
+                    total = jnp.where(tiles[0] == t, 1.0, 0.0) * sources[0]
+                    for k in range(1, 4):
+                        total = total + jnp.where(tiles[k] == t, 1.0, 0.0) * sources[k]
+                    totals.append(total)
+                sums.append(totals)
             for t in range(NT):
-                total = jnp.where(tiles[0] == t, 1.0, 0.0) * sources[0]
-                for k in range(1, 4):
-                    total = total + jnp.where(tiles[k] == t, 1.0, 0.0) * sources[k]
-                high, rest = split(total)
+                high, rest = split(jnp.concatenate([sums[0][t], sums[1][t]], axis=0))
                 whl[rows, t * PH : (t + 1) * PH] = high
                 whl[rest_rows, t * PH : (t + 1) * PH] = rest
             return carry
 
-        lax.fori_loop(0, block_rows, form, 0)
+        lax.fori_loop(0, block_rows // 2, form, 0)
         y = dot(whl[...], tst[...])
-        y = y[:flat] + y[flat:]
-        xs[...] = rhs_ref[...].reshape(flat, PH) + (y[:, :PH] + y[:, PH:])
-
-        def form_diag(i, carry):
-            rows = pl.ds(pl.multiple_of(i * NV, NV), NV)
-            rest_rows = pl.ds(pl.multiple_of(flat + i * NV, NV), NV)
+        y = y[:size] + y[size:]
+        xs[...] = rhs_ref[:, columns, :].reshape(size, PH) + (y[:, :PH] + y[:, PH:])
+
+        def form_diag(pair, carry):
+            rows = pl.ds(pl.multiple_of(pair * NV, NV), NV)
+            rest_rows = pl.ds(pl.multiple_of(size + pair * NV, NV), NV)
             value = xs[rows, :]
             rest = value - value.astype(BF16).astype(F32)
             for t in range(NT):
-                keep = jnp.where(diag_s[i] == t, 1.0, 0.0)
-                whl[rows, t * PH : (t + 1) * PH] = (value * keep).astype(BF16)
-                whl[rest_rows, t * PH : (t + 1) * PH] = (rest * keep).astype(BF16)
+                keep = [jnp.where(diag_s[2 * pair + n] == t, 1.0, 0.0) for n in range(2)]
+                for source, place in ((value, rows), (rest, rest_rows)):
+                    kept = jnp.concatenate(
+                        [source[:HALF] * keep[0], source[HALF:] * keep[1]], axis=0
+                    )
+                    whl[place, t * PH : (t + 1) * PH] = kept.astype(BF16)
             return carry
 
-        lax.fori_loop(0, block_rows, form_diag, 0)
+        lax.fori_loop(0, block_rows // 2, form_diag, 0)
         y = dot(whl[...], ist[...])
-        y = y[:flat] + y[flat:]
-        target[...] = (y[:, :PH] + y[:, PH:]).reshape(block_rows, NV, PH)
+        y = y[:size] + y[size:]
+        target[...] = (y[:, :PH] + y[:, PH:]).reshape(block_rows, HALF, PH)
 
     arrive(meta_s, n_zc - 1, agg_sem.at[0])
     arrive(meta_t, n_xy - 1, agg_sem.at[1])
@@ -344,7 +409,7 @@
         match[rows, :] = jnp.where(column == source_row, 1.0, 0.0).astype(BF16)
         return carry
 
-    lax.fori_loop(0, n_xy, build, 0)
+    lax.fori_loop(0, n_xy, build, 0, unroll=2)
     block_lane = (iota((8, PH), 1) // NV) == iota((8, PH), 0)
     fold = jnp.where(iota((PH, PH), 0) % NV == iota((PH, PH), 1) % NV, 1.0, 0.0).astype(BF16)
 
@@ -366,7 +431,7 @@
                 stage_m[rows, :] = jnp.where(block_lane, value[q : q + 1, :], 0.0)
             return carry
 
-        lax.fori_loop(0, n_zc, spread, 0)
+        lax.fori_loop(0, n_zc, spread, 0, unroll=4)
         both = jnp.concatenate(split(stage_m[...]), axis=1)
         y = dot(match[...], both)
         stage_p[...] = fold_lanes(y[:, :PH] + y[:, PH:])
@@ -377,29 +442,25 @@
                 stage_o[which, d, q : q + 1, :] = to_flat_rows(value, q)
             return carry
 
-        lax.fori_loop(0, n_xy, flatten, 0)
+        lax.fori_loop(0, n_xy, flatten, 0, unroll=4)
         stage_b[which, pl.ds(xy, 1)] = stage_o[which, pl.ds(xy, 1)]
 
         def out_part(step):
-            return stage_o.at[which].at[pl.ds((xy + step) % n_xy, 1)]
+            return stage_o.at[which].at[pl.ds(lax.rem(xy + step, n_xy), 1)]
 
         group_copies(out_part, stage_b.at[which], xy, xy_peer, n_xy, b_sem.at[which])
 
     partial_sums(0)
 
-    arrive(arrived[0], 2 * (n_rows - 1), big_sem.at[0])
-    for copy in band1:
-        copy.wait_recv()
-    coupled_apply(0, first)
-    send_blocks(first, 1)
-    band2 = band_copies(first, low.at[1], up.at[1], band_sem.at[1])
+    for part in range(PARTS):
+        coupled_apply(0, part, field[1][part])
+        send_blocks(1, part)
+        bands[1].append(share_band(1, part))
     ones = jnp.ones((8, PH), BF16)
     rhs_parts = split(rhs_ref[...].reshape(flat, PH))
     rhs_sum = (nt_dot(ones, rhs_parts[0]) + nt_dot(ones, rhs_parts[1]))[0:1, :]
-    arrive(arrived[1], 2 * (n_rows - 1), big_sem.at[1])
-    for copy in band2:
-        copy.wait_recv()
-    coupled_apply(1, out_ref)
+    for part in range(PARTS):
+        coupled_apply(1, part, out_ref.at[:, part * HALF : (part + 1) * HALF, :])
 
     second_parts = split(out_ref[...].reshape(flat, PH))
     projected = nt_dot(cols[...], second_parts[0]) + nt_dot(cols[...], second_parts[1])
@@ -415,12 +476,12 @@
             xhl[1, place, :] = rest
         return carry
 
-    lax.fori_loop(0, n_rows, edge, 0)
+    lax.fori_loop(0, n_rows, edge, 0, unroll=4)
     edges = nt_dot(ones, xhl[0]) + nt_dot(ones, xhl[1])
     for group in range(n_rows // 4):
         send_small[group] = edges[0:1, group * PH : (group + 1) * PH]
     recv_small[0] = edges[0:1, 0:PH]
-    rows_copies(lambda step: send_small.at[pl.ds(step // 4, 1)], recv_small, 1, small_sem, 1)
+    rows_copies(lambda step: send_small.at[pl.ds(lax.div(step, 4), 1)], recv_small, 1, small_sem, 1)
 
     own = projected[16:24] + projected[24:32]
     local_sum = rhs_sum - jnp.sum(jnp.where(sub8 == dflat, own, 0.0), axis=0, keepdims=True)
@@ -445,7 +506,7 @@
         zbuf[i] = total
         return carry
 
-    lax.fori_loop(0, block_rows, collect_edges, 0)
+    lax.fori_loop(0, block_rows, collect_edges, 0, unroll=4)
     rows_of = fold_lanes(zbuf[...].reshape(block_rows, PH))
     for q in range(4):
         res_flat[0, q : q + 1, :] = local_sum[:, q * PH : (q + 1) * PH] + to_flat_rows(rows_of, q)
@@ -466,11 +527,14 @@
     drain(meta_s, n_zc - 1, agg_sem.at[0])
     drain(meta_t, n_xy - 1, agg_sem.at[1])
     for which in range(2):
-        drain(send_big.at[which], 2 * (n_rows - 1), big_sem.at[which])
+        for part in range(PARTS):
+            drain(send_big.at[which].at[part], 2 * (n_rows - 1), big_sem.at[which].at[part])
+            for copy in bands[which][part]:
+                copy.wait_send()
         drain(stage_a.at[which], n_zc - 1, a_sem.at[which])
         drain(stage_o.at[which], n_xy - 1, b_sem.at[which])
     drain(recv_small, n_rows - 1, small_sem)
-    for copy in band1 + band2 + uband:
+    for copy in uband:
         copy.wait_send()
 
 
@@ -497,12 +561,17 @@
     smem = pl.BlockSpec(memory_space=pltpu.SMEM)
     full = pl.BlockSpec(memory_space=pltpu.VMEM)
     scratch = [
+        vmem((block_rows, NV, PH), F32),
+        vmem(diag_table.shape, F32),
+        vmem(diag_table.shape, F32),
+        vmem(diag_table.shape, F32),
+        dma((6,)),
         vmem((NT * PH, 2 * PH), BF16),
         vmem((NT * PH, 2 * PH), BF16),
         vmem((4 * NT, PH), BF16),
         vmem((NT, 1, PH), F32),
-        vmem((2 * flat, NT * PH), BF16),
-        vmem((flat, PH), F32),
+        vmem((flat, NT * PH), BF16),
+        vmem((flat // 2, PH), F32),
         vmem((n_rows, 1, PH), I32),
         vmem((n_rows, 1, PH), I32),
         vmem((1, 1, PH), I32),
@@ -519,12 +588,17 @@
         vmem((n_zc * block_rows, PH), F32),
         vmem((n_xy * block_rows, PH), F32),
         vmem((2, n_xy, 4, PH), F32),
-        vmem((2, 2 * n_rows, NV, PH), F32),
-        vmem((2 * n_rows, NV, PH), F32),
-        vmem((2 * n_rows, NV, PH), F32),
-        vmem((2, block_rows, NV, PH), F32),
-        vmem((2, block_rows, NV, PH), F32),
-        vmem((block_rows, NV, PH), F32),
+        vmem((2, PARTS, 2 * n_rows, HALF, PH), F32),
+        vmem((2 * n_rows, HALF, PH), F32),
+        vmem((2 * n_rows, HALF, PH), F32),
+        vmem((2 * n_rows, HALF, PH), F32),
+        vmem((2 * n_rows, HALF, PH), F32),
+        vmem((2, PARTS, block_rows, HALF, PH), F32),
+        vmem((2, PARTS, block_rows, HALF, PH), F32),
+        vmem((block_rows, HALF, PH), F32),
+        vmem((block_rows, HALF, PH), F32),
+        vmem((block_rows, HALF, PH), F32),
+        vmem((block_rows, HALF, PH), F32),
         vmem((2, 2 * n_rows * NV, PH), BF16),
         vmem((n_rows // 4, 1, PH), F32),
         vmem((n_rows, 1, PH), F32),
@@ -534,8 +608,8 @@
         vmem((block_rows, 1, PH), F32),
         dma((2,)),
         dma((2, 2)),
-        dma((2, 2)),
-        dma((2, 2, 2)),
+        dma((2, PARTS, 2)),
+        dma((2, PARTS, 2, 2)),
         dma((2,)),
         dma((2, 2)),
         dma((2, 2)),
@@ -545,18 +619,18 @@
     return pl.pallas_call(
         functools.partial(kernel, n_band, n_rows),
         out_shape=jax.ShapeDtypeStruct(start_iterate.shape, F32),
-        in_specs=[smem] * 5 + [full] * 5,
+        in_specs=[smem] * 5 + [pl.BlockSpec(memory_space=pl.ANY)] * 5,
         out_specs=full,
         scratch_shapes=scratch,
         compiler_params=pltpu.CompilerParams(
-            collective_id=0, has_side_effects=True, vmem_limit_bytes=48 * 1024 * 1024
+            collective_id=0, has_side_effects=True, vmem_limit_bytes=67043328
         ),
     )(
         diag_index,
-        tile_index,
-        source_owner,
-        source_local,
-        aggregate_map,
+        tile_index.T,
+        source_owner.T,
+        source_local.T,
+        aggregate_map.T,
         start_iterate,
         right_side,
         diag_table,

time: 116 us -> 97.3 us (0.84)
  Pallas kernels: 108 us -> 95.5 us
  local copies, waits for them, and re-layouts: 8.49 us -> 1.67 us
    pallas_call x1, Pallas kernels: 108 us -> 95.5 us  [on_device(): pl.pallas_call(functools.partial(kernel, n_band, n_rows), out_shape=jax.S...]
    unnamed x23 -> x1, local copies, waits for them, and re-layouts: 8.49 us -> 1.67 us
where the time goes in v2:
time: 97.3 us; the launch traced here: 97.1 us
  Pallas kernels  95.5 us (98%)
  local copies, waits for them, and re-layouts  1.67 us (2%)
    pallas_call x1, Pallas kernels, on_device(): pl.pallas_call(functools.partial(kernel, n_band, n_rows), out_shape=jax.S...  95.5 us

profile of v2, /device:TPU:1, one launch (start us, length us, event | category | flops | bytes accessed | tf_op | source)
XLA Modules:
  0.0 97.1 jit_solution(5594569389433312064)
XLA Ops:
  0.0 95.5 %shard_map.100 = f32[32,16,128]{2,1,0:T(8,128)} custom-call(s32[32]{0:T(128)} %diag_s.1, s32[4,32]{1,0:T(4,128)} %bitcast.4, s32[2,32]{1,0:T(2,128)} %bitcast.5, s32[2,32]{1,0:T(2,128)} %bitcast.6, s32[1,32]{1,0:T(1,128)} %bitcast.7, f32[32,16,128]{2,1,0:T(8,128)} %v_hbm.1, f32[32,16,128]{2,1,0:T(8,128)} %rhs_hbm.1, f32[8,128,128]{2,1,0:T(8,128)} %dtab_hbm.1, ...), custom_call_target="tpu_custom_call" | custom-call | tf_op jit(solution)/shard_map/pallas_call | solution.py:619
  95.5 1.7 %copy.12 = f32[32,16,128]{2,1,0:T(8,128)} copy(f32[32,16,128]{2,1,0:T(8,128)} %shard_map.100) | data formatting | bytes 524288

commit v3 on v2

--- a/solution.py
+++ b/solution.py
@@ -59,6 +59,8 @@
     itab,
     ttab,
     in_sem,
+    tile_mask,
+    diag_mask,
     tst,
     ist,
     cols,
@@ -66,7 +68,6 @@
     whl,
     xs,
     msg,
-    recvreq,
     slots_v,
     reqs_s,
     slots_s,
@@ -119,10 +120,30 @@
     b = lax.axis_index("band")
     r = lax.axis_index("rows")
     x = r // n_zc
+    z = (r // CORES) % n_z
+    c = r % CORES
+    n_xc = n_x * CORES
     zc = r % n_zc
     xy = x * n_band + b
     below = (b + n_band - 1) % n_band
     above = (b + 1) % n_band
+
+    def turn_peers(turn, sign):
+        odd = lax.rem(turn, 2)
+        dz = odd * lax.div(turn + 1, 2) + (1 - odd) * (n_z - lax.div(turn, 2))
+        pz = lax.rem(z + sign * dz + 2 * n_z, n_z)
+        peers = []
+        for m in range(n_xc):
+            px = lax.rem(x + sign * (m // CORES) + n_x, n_x)
+            peers.append((px * n_z + pz) * CORES + lax.rem(c + m % CORES, CORES))
+        return peers
+
+    def step_of(owner):
+        dx = lax.rem(x - lax.div(owner, n_zc) + n_x, n_x)
+        dz = lax.rem(z - lax.rem(lax.div(owner, CORES), n_z) + n_z, n_z)
+        dc = lax.rem(c + owner, CORES)
+        turn = jnp.where(dz == 0, 0, jnp.where(2 * dz <= n_z, 2 * dz - 1, 2 * (n_z - dz)))
+        return turn * n_xc + dx * CORES + dc
 
     def zc_peer(step):
         return (b, x * n_zc + lax.rem(zc + step, n_zc))
@@ -149,12 +170,6 @@
 
     barrier = pltpu.get_barrier_semaphore()
 
-    def greet_rows(step, carry):
-        pl.semaphore_signal(barrier, inc=1, device_id=(b, lax.rem(r + step, n_rows)), device_id_type=MESH)
-        return carry
-
-    lax.fori_loop(1, n_rows, greet_rows, 0, unroll=best(n_rows - 1))
-
     def greet_planes(step, carry):
         py = lax.rem(b + 1 + lax.div(step, n_x), n_band)
         px = lax.rem(x + step, n_x)
@@ -162,6 +177,12 @@
         return carry
 
     lax.fori_loop(0, n_x * (n_band - 1), greet_planes, 0, unroll=best(n_x * (n_band - 1)))
+
+    def greet_rows(step, carry):
+        pl.semaphore_signal(barrier, inc=1, device_id=(b, lax.rem(r + step, n_rows)), device_id_type=MESH)
+        return carry
+
+    lax.fori_loop(1, n_rows, greet_rows, 0, unroll=best(n_rows - 1))
 
     sub = iota((n_rows, PH), 0)
     lane = iota((n_rows, PH), 1)
@@ -173,7 +194,7 @@
     def collect(i, carry):
         wants, count, slots, aggs, dflat, lowflat, upflat = carry
         for k in range(2):
-            off = lax.rem(r - owner_s[k, i] + n_rows, n_rows)
+            off = step_of(owner_s[k, i])
             hit = sub == off
             value = jnp.where(is_local, local_s[k, i], tile_s[k, i])
             wants = jnp.where(hit & (count == parity), value, wants)
@@ -195,13 +216,14 @@
     )
     for off in range(n_rows):
         msg[off] = wants[off : off + 1, :]
-    recvreq[0] = wants[0:1, :]
     slots_v[0] = slots
     agg_row[0] = aggs.astype(F32)
     meta_s[pl.ds(zc, 1)] = aggs.astype(F32)[None]
     meta_t[pl.ds(xy, 1)] = aggs.astype(F32)[None]
     slot_copy = pltpu.make_async_copy(slots_v, slots_s, loc_sem.at[0])
     slot_copy.start()
+    req_copy = pltpu.make_async_copy(msg.at[pl.ds(0, 1)], reqs_s.at[pl.ds(0, 1)], loc_sem.at[1])
+    req_copy.start()
 
     for load in loads[:4]:
         load.wait()
@@ -219,23 +241,29 @@
 
     pl.semaphore_wait(barrier, n_rows - 1 + n_x * (n_band - 1))
 
-    def rows_copies(source, target, width, sems, step_sign):
-        def copy(step):
-            peer = lax.rem(r + step_sign * step + n_rows, n_rows)
-            return pltpu.make_async_remote_copy(
-                src_ref=source(step),
-                dst_ref=target.at[pl.ds(step * width, width)],
-                send_sem=sems.at[0],
-                recv_sem=sems.at[1],
-                device_id=(b, peer),
-                device_id_type=MESH,
-            )
-
-        def start(step, carry):
-            copy(step).start()
+    def rows_copies(source, target, width, send_sem, recv_sem, sign, first=0, last=n_z - 1):
+        def start(turn, skip):
+            for m, peer in enumerate(turn_peers(turn, sign)):
+                if m < skip:
+                    continue
+                step = turn * n_xc + m
+                pltpu.make_async_remote_copy(
+                    src_ref=source(step),
+                    dst_ref=target.at[pl.ds(step * width, width)],
+                    send_sem=send_sem,
+                    recv_sem=recv_sem,
+                    device_id=(b, peer),
+                    device_id_type=MESH,
+                ).start()
+
+        def one(n, carry):
+            start(last - n, 0)
             return carry
 
-        lax.fori_loop(1, n_rows, start, 0, unroll=best(n_rows - 1))
+        lowest = max(first, 1)
+        lax.fori_loop(0, last - lowest + 1, one, 0)
+        if first == 0:
+            start(0, 1)
 
     def drain(ref, count, sems):
         part = ref.at[pl.ds(0, count)]
@@ -260,7 +288,10 @@
             copies.append(copy)
         return copies
 
-    rows_copies(lambda step: msg.at[pl.ds(step, 1)], recvreq, 1, req_sem, -1)
+    near = min(3, n_z)
+    request = lambda step: msg.at[pl.ds(step, 1)]
+    rows_copies(request, reqs_s, 1, req_sem.at[0], req_sem.at[2], -1, near, n_z - 1)
+    rows_copies(request, reqs_s, 1, req_sem.at[0], req_sem.at[1], -1, 0, near - 1)
 
     def group_copies(source, target, index, peer_of, count, sems):
         def start(step, carry):
@@ -274,7 +305,7 @@
             ).start()
             return carry
 
-        lax.fori_loop(1, count, start, 0, unroll=best(count - 1))
+        lax.fori_loop(1, count, start, 0, unroll=True)
 
     group_copies(lambda step: agg_row, meta_s, zc, zc_peer, n_zc, agg_sem.at[0])
     group_copies(lambda step: agg_row, meta_t, xy, xy_peer, n_xy, agg_sem.at[1])
@@ -298,13 +329,7 @@
             target[rows, PH : 2 * PH] = rest
         return carry
 
-    arrive(recvreq, n_rows - 1, req_sem)
-    req_copy = pltpu.make_async_copy(recvreq, reqs_s, loc_sem.at[1])
-    req_copy.start()
-    slot_copy.wait()
-    req_copy.wait()
-
-    def send_blocks(which, part):
+    def send_blocks(which, part, first=0, last=n_z - 1):
         source = field[which][part]
         buffer = send_big.at[which].at[part]
 
@@ -313,22 +338,49 @@
                 buffer[2 * off + rank] = source[reqs_s[off, 0, rank]]
             return carry
 
-        lax.fori_loop(0, n_rows, gather, 0, unroll=4)
-        arrived[which][part][0:2] = buffer[0:2]
+        lax.fori_loop(first * n_xc, (last + 1) * n_xc, gather, 0, unroll=4)
+        if first == 0:
+            arrived[which][part][0:2] = buffer[0:2]
+        sems = big_sem.at[which].at[part]
         rows_copies(
             lambda step: buffer.at[pl.ds(2 * step, 2)],
             arrived[which][part],
             2,
-            big_sem.at[which].at[part],
+            sems.at[0],
+            sems.at[1],
             1,
+            first,
+            last,
         )
 
-    for part in range(PARTS):
-        send_blocks(0, part)
+    req_copy.wait()
+    part_near = reqs_s.at[pl.ds(0, near * n_xc - 1)]
+    pltpu.make_async_copy(part_near, part_near, req_sem.at[1]).wait()
+    send_blocks(0, 0, 0, near - 1)
+    part_far = reqs_s.at[pl.ds(0, (n_z - near) * n_xc)]
+    pltpu.make_async_copy(part_far, part_far, req_sem.at[2]).wait()
+    send_blocks(0, 0, near, n_z - 1)
+    send_blocks(0, 1)
+    slot_copy.wait()
     for load in loads[4:]:
         load.wait()
     lax.fori_loop(0, NT, prepare, 0)
     size = block_rows * HALF
+    sub_tile = iota((NT, PH), 0)
+
+    def make_masks(i, carry):
+        tiles = (
+            tile_s[0, i],
+            tile_s[1, i],
+            jnp.where(b == 0, -1, tile_s[2, i]),
+            jnp.where(b == n_band - 1, -1, tile_s[3, i]),
+        )
+        for k in range(4):
+            tile_mask[4 * i + k] = jnp.where(sub_tile == tiles[k], 1.0, 0.0)
+        diag_mask[i] = jnp.where(sub_tile == diag_s[i], 1.0, 0.0)
+        return carry
+
+    lax.fori_loop(0, block_rows, make_masks, 0, unroll=4)
 
     def coupled_apply(which, part, target):
         arrive(arrived[which][part], 2 * (n_rows - 1), big_sem.at[which].at[part])
@@ -347,17 +399,11 @@
                     low[which, part, i],
                     up[which, part, i],
                 )
-                tiles = (
-                    tile_s[0, i],
-                    tile_s[1, i],
-                    jnp.where(b == 0, -1, tile_s[2, i]),
-                    jnp.where(b == n_band - 1, -1, tile_s[3, i]),
-                )
                 totals = []
                 for t in range(NT):
-                    total = jnp.where(tiles[0] == t, 1.0, 0.0) * sources[0]
+                    total = tile_mask[4 * i, t : t + 1, :] * sources[0]
                     for k in range(1, 4):
-                        total = total + jnp.where(tiles[k] == t, 1.0, 0.0) * sources[k]
+                        total = total + tile_mask[4 * i + k, t : t + 1, :] * sources[k]
                     totals.append(total)
                 sums.append(totals)
             for t in range(NT):
@@ -377,7 +423,7 @@
             value = xs[rows, :]
             rest = value - value.astype(BF16).astype(F32)
             for t in range(NT):
-                keep = [jnp.where(diag_s[2 * pair + n] == t, 1.0, 0.0) for n in range(2)]
+                keep = [diag_mask[2 * pair + n, t : t + 1, :] for n in range(2)]
                 for source, place in ((value, rows), (rest, rest_rows)):
                     kept = jnp.concatenate(
                         [source[:HALF] * keep[0], source[HALF:] * keep[1]], axis=0
@@ -481,7 +527,7 @@
     for group in range(n_rows // 4):
         send_small[group] = edges[0:1, group * PH : (group + 1) * PH]
     recv_small[0] = edges[0:1, 0:PH]
-    rows_copies(lambda step: send_small.at[pl.ds(lax.div(step, 4), 1)], recv_small, 1, small_sem, 1)
+    rows_copies(lambda step: send_small.at[pl.ds(lax.div(step, 4), 1)], recv_small, 1, small_sem.at[0], small_sem.at[1], 1)
 
     own = projected[16:24] + projected[24:32]
     local_sum = rhs_sum - jnp.sum(jnp.where(sub8 == dflat, own, 0.0), axis=0, keepdims=True)
@@ -566,13 +612,14 @@
         vmem(diag_table.shape, F32),
         vmem(diag_table.shape, F32),
         dma((6,)),
+        vmem((4 * block_rows, NT, PH), F32),
+        vmem((block_rows, NT, PH), F32),
         vmem((NT * PH, 2 * PH), BF16),
         vmem((NT * PH, 2 * PH), BF16),
         vmem((4 * NT, PH), BF16),
         vmem((NT, 1, PH), F32),
         vmem((flat, NT * PH), BF16),
         vmem((flat // 2, PH), F32),
-        vmem((n_rows, 1, PH), I32),
         vmem((n_rows, 1, PH), I32),
         vmem((1, 1, PH), I32),
         pltpu.SMEM((n_rows, 1, PH), I32),
@@ -606,7 +653,7 @@
         vmem((NT, flat), F32),
         vmem((NT, flat), F32),
         vmem((block_rows, 1, PH), F32),
-        dma((2,)),
+        dma((3,)),
         dma((2, 2)),
         dma((2, PARTS, 2)),
         dma((2, PARTS, 2, 2)),

time: 97.3 us -> 95.4 us (0.980)
  Pallas kernels: 95.5 us -> 93.6 us
    pallas_call x1, Pallas kernels: 95.5 us -> 93.6 us  [on_device(): pl.pallas_call(functools.partial(kernel, n_band, n_rows), out_shape=jax.S...]
where the time goes in v3:
time: 95.4 us; the launch traced here: 95.2 us
  Pallas kernels  93.6 us (98%)
  local copies, waits for them, and re-layouts  1.67 us (2%)
    pallas_call x1, Pallas kernels, on_device(): pl.pallas_call(functools.partial(kernel, n_band, n_rows), out_shape=jax.S...  93.6 us

profile of v3, /device:TPU:1, one launch (start us, length us, event | category | flops | bytes accessed | tf_op | source)
XLA Modules:
  0.0 95.2 jit_solution(5291419016283622501)
XLA Ops:
  0.0 93.6 %shard_map.100 = f32[32,16,128]{2,1,0:T(8,128)} custom-call(s32[32]{0:T(128)} %diag_s.1, s32[4,32]{1,0:T(4,128)} %bitcast.4, s32[2,32]{1,0:T(2,128)} %bitcast.5, s32[2,32]{1,0:T(2,128)} %bitcast.6, s32[1,32]{1,0:T(1,128)} %bitcast.7, f32[32,16,128]{2,1,0:T(8,128)} %v_hbm.1, f32[32,16,128]{2,1,0:T(8,128)} %rhs_hbm.1, f32[8,128,128]{2,1,0:T(8,128)} %dtab_hbm.1, ...), custom_call_target="tpu_custom_call" | custom-call | tf_op jit(solution)/shard_map/pallas_call | solution.py:666
  93.6 1.7 %copy.12 = f32[32,16,128]{2,1,0:T(8,128)} copy(f32[32,16,128]{2,1,0:T(8,128)} %shard_map.100) | data formatting | bytes 524288

commit v4 on v3

--- a/solution.py
+++ b/solution.py
@@ -43,11 +43,11 @@
 def kernel(
     n_band,
     n_rows,
-    diag_s,
-    tile_s,
-    owner_s,
-    local_s,
-    agg_s,
+    diag_hbm,
+    tile_hbm,
+    owner_hbm,
+    local_hbm,
+    agg_hbm,
     v_hbm,
     rhs_hbm,
     dtab_hbm,
@@ -59,6 +59,12 @@
     itab,
     ttab,
     in_sem,
+    diag_s,
+    tile_s,
+    owner_s,
+    local_s,
+    agg_s,
+    index_sem,
     tile_mask,
     diag_mask,
     tst,
@@ -165,7 +171,19 @@
             )
         )
     ]
-    for load in loads:
+    index_loads = [
+        pltpu.make_async_copy(source, target, index_sem.at[n])
+        for n, (source, target) in enumerate(
+            (
+                (diag_hbm, diag_s),
+                (tile_hbm, tile_s),
+                (owner_hbm, owner_s),
+                (local_hbm, local_s),
+                (agg_hbm, agg_s),
+            )
+        )
+    ]
+    for load in index_loads + loads:
         load.start()
 
     barrier = pltpu.get_barrier_semaphore()
@@ -184,6 +202,8 @@
 
     lax.fori_loop(1, n_rows, greet_rows, 0, unroll=best(n_rows - 1))
 
+    for load in index_loads:
+        load.wait()
     sub = iota((n_rows, PH), 0)
     lane = iota((n_rows, PH), 1)
     lane1 = iota((1, PH), 1)
@@ -508,11 +528,6 @@
     for part in range(PARTS):
         coupled_apply(1, part, out_ref.at[:, part * HALF : (part + 1) * HALF, :])
 
-    second_parts = split(out_ref[...].reshape(flat, PH))
-    projected = nt_dot(cols[...], second_parts[0]) + nt_dot(cols[...], second_parts[1])
-    u_send[...] = projected[0:8] + projected[8:16]
-    uband = band_copies(u_send, u_low, u_up, uband_sem)
-
     def edge(off, carry):
         for rank in range(2):
             value = out_ref[reqs_s[off, 0, rank]] * colt[reqs_s[off, 0, 2 + rank]]
@@ -522,12 +537,17 @@
             xhl[1, place, :] = rest
         return carry
 
-    lax.fori_loop(0, n_rows, edge, 0, unroll=4)
+    lax.fori_loop(0, n_rows, edge, 0, unroll=8)
     edges = nt_dot(ones, xhl[0]) + nt_dot(ones, xhl[1])
     for group in range(n_rows // 4):
         send_small[group] = edges[0:1, group * PH : (group + 1) * PH]
     recv_small[0] = edges[0:1, 0:PH]
     rows_copies(lambda step: send_small.at[pl.ds(lax.div(step, 4), 1)], recv_small, 1, small_sem.at[0], small_sem.at[1], 1)
+
+    second_parts = split(out_ref[...].reshape(flat, PH))
+    projected = nt_dot(cols[...], second_parts[0]) + nt_dot(cols[...], second_parts[1])
+    u_send[...] = projected[0:8] + projected[8:16]
+    uband = band_copies(u_send, u_low, u_up, uband_sem)
 
     own = projected[16:24] + projected[24:32]
     local_sum = rhs_sum - jnp.sum(jnp.where(sub8 == dflat, own, 0.0), axis=0, keepdims=True)
@@ -552,7 +572,7 @@
         zbuf[i] = total
         return carry
 
-    lax.fori_loop(0, block_rows, collect_edges, 0, unroll=4)
+    lax.fori_loop(0, block_rows, collect_edges, 0, unroll=8)
     rows_of = fold_lanes(zbuf[...].reshape(block_rows, PH))
     for q in range(4):
         res_flat[0, q : q + 1, :] = local_sum[:, q * PH : (q + 1) * PH] + to_flat_rows(rows_of, q)
@@ -604,7 +624,6 @@
     flat = block_rows * NV
     vmem = pltpu.VMEM
     dma = pltpu.SemaphoreType.DMA
-    smem = pl.BlockSpec(memory_space=pltpu.SMEM)
     full = pl.BlockSpec(memory_space=pltpu.VMEM)
     scratch = [
         vmem((block_rows, NV, PH), F32),
@@ -612,6 +631,12 @@
         vmem(diag_table.shape, F32),
         vmem(diag_table.shape, F32),
         dma((6,)),
+        pltpu.SMEM(diag_index.shape, I32),
+        pltpu.SMEM(tile_index.shape[::-1], I32),
+        pltpu.SMEM(source_owner.shape[::-1], I32),
+        pltpu.SMEM(source_local.shape[::-1], I32),
+        pltpu.SMEM(aggregate_map.shape[::-1], I32),
+        dma((5,)),
         vmem((4 * block_rows, NT, PH), F32),
         vmem((block_rows, NT, PH), F32),
         vmem((NT * PH, 2 * PH), BF16),
@@ -666,7 +691,7 @@
     return pl.pallas_call(
         functools.partial(kernel, n_band, n_rows),
         out_shape=jax.ShapeDtypeStruct(start_iterate.shape, F32),
-        in_specs=[smem] * 5 + [pl.BlockSpec(memory_space=pl.ANY)] * 5,
+        in_specs=[pl.BlockSpec(memory_space=pl.ANY)] * 10,
         out_specs=full,
         scratch_shapes=scratch,
         compiler_params=pltpu.CompilerParams(

time: 95.4 us -> 94.9 us (level)
  no operation moved by 1% of the time
where the time goes in v4:
time: 94.9 us; the launch traced here: 94.8 us
  Pallas kernels  93.1 us (98%)
  local copies, waits for them, and re-layouts  1.67 us (2%)
    pallas_call x1, Pallas kernels, on_device(): pl.pallas_call(functools.partial(kernel, n_band, n_rows), out_shape=jax.S...  93.1 us

profile of v4, /device:TPU:1, one launch (start us, length us, event | category | flops | bytes accessed | tf_op | source)
XLA Modules:
  0.0 94.8 jit_solution(17611094840544749215)
XLA Ops:
  0.0 93.1 %shard_map.100 = f32[32,16,128]{2,1,0:T(8,128)} custom-call(s32[32]{0:T(128)} %diag_hbm.1, s32[4,32]{1,0:T(4,128)} %bitcast.4, s32[2,32]{1,0:T(2,128)} %bitcast.5, s32[2,32]{1,0:T(2,128)} %bitcast.6, s32[1,32]{1,0:T(1,128)} %bitcast.7, f32[32,16,128]{2,1,0:T(8,128)} %v_hbm.1, f32[32,16,128]{2,1,0:T(8,128)} %rhs_hbm.1, f32[8,128,128]{2,1,0:T(8,128)} %dtab_hbm.1, ...), custom_call_target="tpu_custom_call" | custom-call | tf_op jit(solution)/shard_map/pallas_call | solution.py:691
  93.1 1.7 %copy.12 = f32[32,16,128]{2,1,0:T(8,128)} copy(f32[32,16,128]{2,1,0:T(8,128)} %shard_map.100) | data formatting | bytes 524288
